TPU v7x, 32 devices: a whole 2x2x4 slice. The times are simulated.
32 devices in a mesh: groups: 2 (over x), row: 8 (over z, y), col: 2 (over core).
Axes of the slice: x: 2, y: 2, z: 4, core: 2. Of those that a mesh axis runs over, the one named last changes fastest.
Arguments:
- spectra: bfloat16 [4096, 16384], P(('groups', 'row', 'col')), parts along dimension 0, may hold values from -60 to 60
- block_order: int32 [4096], P('groups'), parts along dimension 0, may hold values from 0 to 2047, each once
- offsets: int32 [17], replicated, may hold values from -24 to 24, as said below
Outputs:
- similarity: float32 [4096, 2048], P(('groups', 'row', 'col')), parts along dimension 0
There are 2 independent parts, one for each index of `groups`. A program takes and returns all parts, laid end to end along the dimension named above; an argument that names none is the same for every part. Nothing has to cross between parts.
Inputs may be any that keep to these rules, and one draw needn't show every extreme that they name: `offsets`: the 17 values are distinct, include 0 and 24, and the negative of each value is also among them.
All inputs are finite; a program needn't handle non-finite values.
Results may differ from a plain program's by a relative error of at most 0.0013.
Values may be sent and summed in bfloat16 or wider, within the bound.
A program may use at most 128 MiB of HBM per device.

v0:
```python
import math
import jax
import jax.numpy as jnp
from jax import lax
from jax.sharding import PartitionSpec as P

TAPS = 16
PADW = 64


def taps_table(count):
    steps = jnp.arange(count, dtype=jnp.float32)
    return (0.5 - 0.5 * jnp.cos(2.0 * math.pi * (steps + 0.5) / count)).astype(jnp.bfloat16)


def shifted_stack(mine, offsets):
    coarse_len = mine.shape[1]
    mine_padded = jnp.pad(mine, ((0, 0), (PADW, PADW)))

    def moved(offset):
        return lax.dynamic_slice_in_dim(mine_padded, PADW - offset, coarse_len, 1)

    stacked = jax.vmap(moved)(offsets)
    return stacked.reshape(-1, coarse_len)


def strip_scores(stacked, extended, first_block, block_rows, width_blocks):
    panel = lax.dynamic_slice_in_dim(
        extended, first_block * block_rows, width_blocks * block_rows, 0
    )
    scores = lax.dot_general(
        stacked, panel, (((1,), (1,)), ((), ())), preferred_element_type=jnp.float32
    )
    scores = scores.reshape(-1, block_rows, width_blocks, block_rows)
    return jnp.max(scores, axis=0)


def per_device(spectra, block_order, offsets):
    block_rows, bins = spectra.shape
    coarse_len = bins // TAPS
    group = min(128, coarse_len)
    weights = jnp.kron(
        jnp.eye(group, dtype=jnp.float32), taps_table(TAPS).astype(jnp.float32)[:, None]
    ).astype(jnp.bfloat16)
    windows = spectra.reshape(block_rows * coarse_len // group, TAPS * group)
    coarse = jnp.dot(windows, weights, preferred_element_type=jnp.float32).reshape(
        block_rows, coarse_len
    )
    scale = lax.rsqrt(jnp.mean(coarse * coarse, axis=1, keepdims=True) + 1e-06) * (
        1.0 / math.sqrt(coarse_len)
    )
    unit = (coarse * scale).astype(jnp.bfloat16)
    every = lax.all_gather(unit, ("row", "col"), axis=0, tiled=True)
    ordered = jnp.take(every, block_order, axis=0)
    total_rows = ordered.shape[0]
    blocks = lax.axis_size("row") * lax.axis_size("col")
    myself = lax.axis_index("row") * lax.axis_size("col") + lax.axis_index("col")
    mine = lax.dynamic_slice_in_dim(ordered, myself * block_rows, block_rows, 0)
    stacked = shifted_stack(mine, offsets)
    extended = jnp.concatenate([ordered, ordered[:block_rows]], axis=0)
    empty = jnp.zeros((blocks, block_rows, block_rows), jnp.float32)

    def place(acc, first):
        scores = strip_scores(stacked, extended, first, block_rows, 2)
        acc = lax.dynamic_update_slice_in_dim(acc, scores[None, :, 0, :], first, 0)
        return lax.dynamic_update_slice_in_dim(acc, scores[None, :, 1, :], (first + 1) % blocks, 0)

    result = lax.fori_loop(0, blocks // 2, lambda pair, acc: place(acc, 2 * pair), empty)
    return jnp.transpose(result, (1, 0, 2)).reshape(block_rows, total_rows)


def solution(mesh):
    in_specs = (P(("groups", "row", "col"), None), P("groups"), P())
    out_specs = P(("groups", "row", "col"), None)
    return jax.shard_map(
        per_device, mesh=mesh, in_specs=in_specs, out_specs=out_specs, check_vma=False
    )
```

profile of v0, /device:TPU:0, one launch (start us, length us, event | category | flops | bytes accessed | tf_op | source)
XLA Modules:
  0.0 212.4 jit_solution(15265125319011555981)
XLA Ops:
  6.6 7.4 %reshape.96 = bf16[1024,2048]{1,0:T(8,128)(2,1)} reshape(bf16[128,16384]{1,0:T(8,128)(2,1)} %param.5) | data formatting | bytes 8388608 | tf_op jit(solution)/shard_map/reshape | solution.py:45
  14.2 3.7 %multiply_reduce_fusion = (f32[1024]{0:T(1024)S(1)}, f32[1024,128]{0,1:T(8,128)S(1)}) fusion(bf16[2048,128]{1,0:T(8,128)(2,1)S(1)} %bitcast.40, bf16[1024,2048]{1,0:T(8,128)(2,1)} %reshape.96), kind=kOutput, calls=%fused_computation.14 | convolution fusion | flops 537132032 | bytes 5246976 | tf_op jit(solution)/shard_map/dot_general | solution.py:46
  18.4 0.8 multiply_convert_fusion.1
  19.4 53.3 %all-gather.2.cloned.1.call-done = bf16[2048,1024]{1,0:T(8,128)(2,1)} async-done(((bf16[128,1024]{1,0:T(8,128)(2,1)}), bf16[2048,1024]{1,0:T(8,128)(2,1)}) %all-gather.2.cloned.1.call-update) | async-done | bytes 4194320 | tf_op jit(solution)/shard_map/all_gather | solution.py:53
  72.7 13.7 %gather_fusion = bf16[2048,1024]{1,0:T(8,128)(2,1)} fusion(bf16[2048,1024]{1,0:T(8,128)(2,1)} %all-gather.2.cloned.1.call-done, s32[2048]{0:T(1024)S(1)} %fusion.3), kind=kCustom, calls=%fused_computation | custom fusion | bytes 8396800 | tf_op jit(solution)/shard_map/jit(_take)/gather | solution.py:54
  86.4 2.5 %broadcast_select_fusion = bf16[2048,1024]{1,0:T(8,128)(2,1)S(1)} fusion(bf16[2048,1024]{1,0:T(8,128)(2,1)} %gather_fusion, pred[2048]{0:T(1024)(128)(4,1)S(1)} %compare_and_fusion), kind=kLoop, calls=%fused_computation.9 | loop fusion | flops 2097152 | bytes 8390656 | tf_op jit(solution)/shard_map/jit(_take)/select_n | solution.py:54
  89.0 2.5 %pad_maximum_fusion = bf16[2176,1024]{1,0:T(8,128)(2,1)} fusion(bf16[128,1024]{1,0:T(8,128)(2,1)S(1)} %get-tuple-element.145, bf16[2048,1024]{1,0:T(8,128)(2,1)S(1)} %broadcast_select_fusion), kind=kLoop, calls=%fused_computation.8 | loop fusion | flops 8912896 | bytes 8912896 | tf_op jit(solution)/shard_map/concatenate | solution.py:60
  91.7 35.6 %while.17 = (s32[]{:T(128)}, bf16[128,1152]{1,0:T(8,128)(2,1)S(1)}, s32[17,2]{0,1:T(2,128)S(1)}, bf16[17,128,1024]{2,1,0:T(8,128)(2,1)}, s32[]{:T(128)}) while((s32[]{:T(128)}, bf16[128,1152]{1,0:T(8,128)(2,1)S(1)}, s32[17,2]{0,1:T(2,128)S(1)}, bf16[17,128,1024]{2,1,0:T(8,128)(2,1)}, s32[]{:T(128)}) %tuple.52), condition=%wide.while_cond, body=%wide.while_body.sunk | while | flops 2 | bytes 525401 | solution.py:21
  91.7 0.5 slice.48
  92.3 1.5 bitcast_dynamic-update-slice_fusion.8
  94.3 1.5 bitcast_dynamic-update-slice_fusion.8
  96.4 1.5 bitcast_dynamic-update-slice_fusion.8
  98.5 1.5 bitcast_dynamic-update-slice_fusion.8
  100.6 1.5 bitcast_dynamic-update-slice_fusion.8
  102.2 0.5 slice.48
  102.7 1.5 bitcast_dynamic-update-slice_fusion.8
  104.8 1.5 bitcast_dynamic-update-slice_fusion.8
  106.9 1.5 bitcast_dynamic-update-slice_fusion.8
  108.5 0.5 slice.48
  109.0 1.5 bitcast_dynamic-update-slice_fusion.8
  111.1 1.5 bitcast_dynamic-update-slice_fusion.8
  113.2 1.5 bitcast_dynamic-update-slice_fusion.8
  114.8 0.5 slice.48
  115.3 1.5 bitcast_dynamic-update-slice_fusion.8
  117.4 1.5 bitcast_dynamic-update-slice_fusion.8
  119.4 1.5 bitcast_dynamic-update-slice_fusion.8
  121.5 1.5 bitcast_dynamic-update-slice_fusion.8
  123.1 0.5 slice.48
  123.6 1.5 bitcast_dynamic-update-slice_fusion.8
  125.7 1.5 bitcast_dynamic-update-slice_fusion.8
  127.3 77.2 %while.16 = (s32[]{:T(128)}, f32[16,128,128]{2,1,0:T(8,128)S(1)}, bf16[2176,1024]{1,0:T(8,128)(2,1)}, bf16[2176,1024]{1,0:T(8,128)(2,1)}, s32[]{:T(128)}, /*inde...) while((s32[]{:T(128)}, f32[16,128,128]{2,1,0:T(8,128)S(1)}, ...), condition=%wide.region_4.5_spmd, body=%wide.region_2.4_spmd.sunk | while | flops 1141374976 | bytes 19005812 | solution.py:68
  127.4 3.9 %convolution_bitcast_fusion.3 = f32[2176,256]{0,1:T(8,128)S(1)} fusion(bf16[2176,1024]{1,0:T(8,128)(2,1)} %get-tuple-element.244, bf16[2176,1024]{1,0:T(8,128)(2,1)} %get-tuple-element.243, s32[]{:T(128)S(6)} %select_n.83), kind=kOutput, calls=%fused_computation.1.clone.1 | convolution fusion | flops 1140850688 | bytes 7208964 | tf_op jit(solution)/shard_map/while/body/eval_jaxpr/dot_general | solution.py:31
  131.2 2.0 copy.14
  133.2 2.7 %reshape.129 = f32[17,128,2,128]{3,2,1,0:T(2,128)S(1)} reshape(f32[2176,256]{1,0:T(8,128)} %copy.14) | data formatting | bytes 4456448 | tf_op jit(solution)/shard_map/while/body/eval_jaxpr/reshape | solution.py:34
  135.9 0.9 reduce_max.17
  137.0 3.9 %convolution_bitcast_fusion.3 = f32[2176,256]{0,1:T(8,128)S(1)} fusion(bf16[2176,1024]{1,0:T(8,128)(2,1)} %get-tuple-element.244, bf16[2176,1024]{1,0:T(8,128)(2,1)} %get-tuple-element.243, s32[]{:T(128)S(6)} %select_n.83), kind=kOutput, calls=%fused_computation.1.clone.1 | convolution fusion | flops 1140850688 | bytes 7208964 | tf_op jit(solution)/shard_map/while/body/eval_jaxpr/dot_general | solution.py:31
  140.9 2.0 copy.14
  142.8 2.7 %reshape.129 = f32[17,128,2,128]{3,2,1,0:T(2,128)S(1)} reshape(f32[2176,256]{1,0:T(8,128)} %copy.14) | data formatting | bytes 4456448 | tf_op jit(solution)/shard_map/while/body/eval_jaxpr/reshape | solution.py:34
  145.6 0.9 reduce_max.17
  146.7 3.9 %convolution_bitcast_fusion.3 = f32[2176,256]{0,1:T(8,128)S(1)} fusion(bf16[2176,1024]{1,0:T(8,128)(2,1)} %get-tuple-element.244, bf16[2176,1024]{1,0:T(8,128)(2,1)} %get-tuple-element.243, s32[]{:T(128)S(6)} %select_n.83), kind=kOutput, calls=%fused_computation.1.clone.1 | convolution fusion | flops 1140850688 | bytes 7208964 | tf_op jit(solution)/shard_map/while/body/eval_jaxpr/dot_general | solution.py:31
  150.5 2.0 copy.14
  152.5 2.7 %reshape.129 = f32[17,128,2,128]{3,2,1,0:T(2,128)S(1)} reshape(f32[2176,256]{1,0:T(8,128)} %copy.14) | data formatting | bytes 4456448 | tf_op jit(solution)/shard_map/while/body/eval_jaxpr/reshape | solution.py:34
  155.2 0.9 reduce_max.17
  156.3 3.9 %convolution_bitcast_fusion.3 = f32[2176,256]{0,1:T(8,128)S(1)} fusion(bf16[2176,1024]{1,0:T(8,128)(2,1)} %get-tuple-element.244, bf16[2176,1024]{1,0:T(8,128)(2,1)} %get-tuple-element.243, s32[]{:T(128)S(6)} %select_n.83), kind=kOutput, calls=%fused_computation.1.clone.1 | convolution fusion | flops 1140850688 | bytes 7208964 | tf_op jit(solution)/shard_map/while/body/eval_jaxpr/dot_general | solution.py:31
  160.2 2.0 copy.14
  162.1 2.7 %reshape.129 = f32[17,128,2,128]{3,2,1,0:T(2,128)S(1)} reshape(f32[2176,256]{1,0:T(8,128)} %copy.14) | data formatting | bytes 4456448 | tf_op jit(solution)/shard_map/while/body/eval_jaxpr/reshape | solution.py:34
  164.9 0.9 reduce_max.17
  165.9 3.9 %convolution_bitcast_fusion.3 = f32[2176,256]{0,1:T(8,128)S(1)} fusion(bf16[2176,1024]{1,0:T(8,128)(2,1)} %get-tuple-element.244, bf16[2176,1024]{1,0:T(8,128)(2,1)} %get-tuple-element.243, s32[]{:T(128)S(6)} %select_n.83), kind=kOutput, calls=%fused_computation.1.clone.1 | convolution fusion | flops 1140850688 | bytes 7208964 | tf_op jit(solution)/shard_map/while/body/eval_jaxpr/dot_general | solution.py:31
  169.8 2.0 copy.14
  171.8 2.7 %reshape.129 = f32[17,128,2,128]{3,2,1,0:T(2,128)S(1)} reshape(f32[2176,256]{1,0:T(8,128)} %copy.14) | data formatting | bytes 4456448 | tf_op jit(solution)/shard_map/while/body/eval_jaxpr/reshape | solution.py:34
  174.5 0.9 reduce_max.17
  175.6 3.9 %convolution_bitcast_fusion.3 = f32[2176,256]{0,1:T(8,128)S(1)} fusion(bf16[2176,1024]{1,0:T(8,128)(2,1)} %get-tuple-element.244, bf16[2176,1024]{1,0:T(8,128)(2,1)} %get-tuple-element.243, s32[]{:T(128)S(6)} %select_n.83), kind=kOutput, calls=%fused_computation.1.clone.1 | convolution fusion | flops 1140850688 | bytes 7208964 | tf_op jit(solution)/shard_map/while/body/eval_jaxpr/dot_general | solution.py:31
  179.5 2.0 copy.14
  181.4 2.7 %reshape.129 = f32[17,128,2,128]{3,2,1,0:T(2,128)S(1)} reshape(f32[2176,256]{1,0:T(8,128)} %copy.14) | data formatting | bytes 4456448 | tf_op jit(solution)/shard_map/while/body/eval_jaxpr/reshape | solution.py:34
  184.2 0.9 reduce_max.17
  185.2 3.9 %convolution_bitcast_fusion.3 = f32[2176,256]{0,1:T(8,128)S(1)} fusion(bf16[2176,1024]{1,0:T(8,128)(2,1)} %get-tuple-element.244, bf16[2176,1024]{1,0:T(8,128)(2,1)} %get-tuple-element.243, s32[]{:T(128)S(6)} %select_n.83), kind=kOutput, calls=%fused_computation.1.clone.1 | convolution fusion | flops 1140850688 | bytes 7208964 | tf_op jit(solution)/shard_map/while/body/eval_jaxpr/dot_general | solution.py:31
  189.1 2.0 copy.14
  191.1 2.7 %reshape.129 = f32[17,128,2,128]{3,2,1,0:T(2,128)S(1)} reshape(f32[2176,256]{1,0:T(8,128)} %copy.14) | data formatting | bytes 4456448 | tf_op jit(solution)/shard_map/while/body/eval_jaxpr/reshape | solution.py:34
  193.8 0.9 reduce_max.17
  194.9 3.9 %convolution_bitcast_fusion.3 = f32[2176,256]{0,1:T(8,128)S(1)} fusion(bf16[2176,1024]{1,0:T(8,128)(2,1)} %get-tuple-element.244, bf16[2176,1024]{1,0:T(8,128)(2,1)} %get-tuple-element.243, s32[]{:T(128)S(6)} %select_n.83), kind=kOutput, calls=%fused_computation.1.clone.1 | convolution fusion | flops 1140850688 | bytes 7208964 | tf_op jit(solution)/shard_map/while/body/eval_jaxpr/dot_general | solution.py:31
  198.8 2.0 copy.14
  200.7 2.7 %reshape.129 = f32[17,128,2,128]{3,2,1,0:T(2,128)S(1)} reshape(f32[2176,256]{1,0:T(8,128)} %copy.14) | data formatting | bytes 4456448 | tf_op jit(solution)/shard_map/while/body/eval_jaxpr/reshape | solution.py:34
  203.5 0.9 reduce_max.17
  204.5 1.1 copy_bitcast_fusion
  (75 shorter events, 9.4 us)
Async XLA Ops:
  6.5 66.1 %all-gather.2.cloned.1.call-start = ((), (), s32[]{:S(2)}) async-start(), calls=%async_computation | async-start | bytes 4456448 | tf_op jit(solution)/shard_map/all_gather | solution.py:53
  14.2 5.1 %copy-start.1 = (s32[17]{0:T(128)S(1)}, s32[17]{0:T(128)}, u32[]{:S(2)}) copy-start(s32[17]{0:T(128)} %param.7) | copy-start | bytes 208
  14.2 5.2 %copy-start = (s32[2048]{0:T(1024)S(1)}, s32[2048]{0:T(1024)}, u32[]{:S(2)}) copy-start(s32[2048]{0:T(1024)} %param.6) | copy-start | bytes 24580
Sparse Core Ops, SparseCore 0:
  19.4 53.2 all-gather.1
where the time goes:
time: 213 us; the launch traced here: 212 us
  local copies, waits for them, and re-layouts  97.1 us (46%)
  waiting for transfers between devices  53.3 us (25%)
  matrix products  34.6 us (16%)
  between operations  13.6 us (6%)
  other arithmetic  13 us (6%)
    all_gather x1, waiting for transfers between devices, per_device(): every = lax.all_gather(unit, ('row', 'col'), axis=0, tiled=True)  53.3 us
    gather x51, local copies, waits for them, and re-layouts  35.5 us
    dot_general x8, matrix products, strip_scores(): lax.dot_general(stacked, panel, (((1,), (1,)), ((), ())), preferred_eleme...  30.8 us
    reshape x8, local copies, waits for them, and re-layouts, strip_scores(): scores = scores.reshape(-1, block_rows, width_blocks, block_rows)  22 us
    dot_general x8, local copies, waits for them, and re-layouts, strip_scores(): lax.dot_general(stacked, panel, (((1,), (1,)), ((), ())), preferred_eleme...  15.8 us
    gather x1, local copies, waits for them, and re-layouts, per_device(): ordered = jnp.take(every, block_order, axis=0)  13.7 us
    reshape x1, local copies, waits for them, and re-layouts, per_device(): windows = spectra.reshape(block_rows * coarse_len // group, TAPS * group)  7.39 us
    reduce_max x8, other arithmetic, strip_scores(): return jnp.max(scores, axis=0)  6.83 us
  transfers between devices with their start and end apart: 1, of which 1 were waited for; matrix products, arithmetic and copies ran while one was open for 0% of the time, Pallas kernels for 0%

commit v1 on v0

--- a/solution.py
+++ b/solution.py
@@ -6,6 +6,36 @@
 
 TAPS = 16
 PADW = 64
+
+
+def perform_strings(u_in, lane_axis):
+    step_out = lax.psum(1, axis_name=lane_axis)
+    left_arr = lax.axis_index(lane_axis)
+    f_now, state_next, answer = (step_out, left_arr, u_in.shape[0])
+    arr_out = lax.dynamic_update_slice_in_dim(
+        jnp.zeros([h * f_now if dev == 0 else h for dev, h in enumerate(u_in.shape)], u_in.dtype),
+        u_in,
+        state_next * answer,
+        axis=0,
+    )
+    val = far_arr = u_in
+    for t in range(1, f_now // 2 + 1):
+        val = lax.ppermute(
+            val, axis_name=lane_axis, perm=[(dev, (dev + 1) % f_now) for dev in range(f_now)]
+        )
+        arr_out = lax.dynamic_update_slice_in_dim(
+            arr_out, val, (state_next - t) % f_now * answer, axis=0
+        )
+        if 2 * t < f_now:
+            far_arr = lax.ppermute(
+                far_arr,
+                axis_name=lane_axis,
+                perm=[(dev, (dev - 1) % f_now) for dev in range(f_now)],
+            )
+            arr_out = lax.dynamic_update_slice_in_dim(
+                arr_out, far_arr, (state_next + t) % f_now * answer, axis=0
+            )
+    return arr_out
 
 
 def taps_table(count):
@@ -50,7 +80,7 @@
         1.0 / math.sqrt(coarse_len)
     )
     unit = (coarse * scale).astype(jnp.bfloat16)
-    every = lax.all_gather(unit, ("row", "col"), axis=0, tiled=True)
+    every = perform_strings(unit, ("row", "col"))
     ordered = jnp.take(every, block_order, axis=0)
     total_rows = ordered.shape[0]
     blocks = lax.axis_size("row") * lax.axis_size("col")

time: 213 us -> 222 us (1.042)
  starting transfers between devices: 0.01 us -> 32 us
  waiting for transfers between devices: 53.3 us -> 27.2 us
  between operations: 13.6 us -> 0.51 us
  local copies, waits for them, and re-layouts: 97.1 us -> 110 us
  other arithmetic: 13 us -> 15.3 us
    all_gather x1 -> x0, waiting for transfers between devices: 53.3 us -> none  [per_device(): every = lax.all_gather(unit, ('row', 'col'), axis=0, tiled=True)]
    ppermute x0 -> x15, starting transfers between devices: none -> 32 us  [the longest x7 31.5 us: perform_strings(): lax.ppermute(far_arr, axis_name=lane_axis, perm=[(dev, (dev - 1) % f_now)...]
    ppermute x0 -> x15, waiting for transfers between devices: none -> 27.2 us  [the longest x8 27.1 us: perform_strings(): lax.ppermute(val, axis_name=lane_axis, perm=[(dev, (dev + 1) % f_now) for...]
    dynamic_update_slice x0 -> x15, local copies, waits for them, and re-layouts: none -> 10.9 us  [the longest x8 5.78 us: perform_strings(): lax.dynamic_update_slice_in_dim(arr_out, val, (state_next - t) % f_now *...]
    broadcast_in_dim x0 -> x1, local copies, waits for them, and re-layouts: none -> 2.56 us  [perform_strings(): jnp.zeros([h * f_now if dev == 0 else h for dev, h in enumerate(u_in.shap...]
    concatenate x1, other arithmetic: 2.52 us -> 4.77 us  [per_device(): extended = jnp.concatenate([ordered, ordered[:block_rows]], axis=0)]
    gather x51, local copies, waits for them, and re-layouts: 35.5 us -> 33.3 us
  transfers between devices with their start and end apart: 1 -> 15, of which waited for: 1 -> 8; matrix products, arithmetic and copies ran while one was open for 0% -> 5% of each run, Pallas kernels for 0% -> 0%
where the time goes in v1:
time: 222 us; the launch traced here: 221 us
  local copies, waits for them, and re-layouts  110 us (50%)
  matrix products  34.6 us (16%)
  starting transfers between devices  32 us (14%)
  waiting for transfers between devices  27.2 us (12%)
  other arithmetic  15.3 us (7%)
    gather x51, local copies, waits for them, and re-layouts  33.3 us
    ppermute x7, starting transfers between devices, perform_strings(): lax.ppermute(far_arr, axis_name=lane_axis, perm=[(dev, (dev - 1) % f_now)...  31.5 us
    dot_general x8, matrix products, strip_scores(): lax.dot_general(stacked, panel, (((1,), (1,)), ((), ())), preferred_eleme...  30.8 us
    ppermute x8, waiting for transfers between devices, perform_strings(): lax.ppermute(val, axis_name=lane_axis, perm=[(dev, (dev + 1) % f_now) for...  27.1 us
    reshape x8, local copies, waits for them, and re-layouts, strip_scores(): scores = scores.reshape(-1, block_rows, width_blocks, block_rows)  22 us
    dot_general x8, local copies, waits for them, and re-layouts, strip_scores(): lax.dot_general(stacked, panel, (((1,), (1,)), ((), ())), preferred_eleme...  15.7 us
    gather x1, local copies, waits for them, and re-layouts, per_device(): ordered = jnp.take(every, block_order, axis=0)  13.7 us
    reshape x1, local copies, waits for them, and re-layouts, per_device(): windows = spectra.reshape(block_rows * coarse_len // group, TAPS * group)  7.41 us
  transfers between devices with their start and end apart: 15, of which 8 were waited for; matrix products, arithmetic and copies ran while one was open for 5% of the time, Pallas kernels for 0%

profile of v1, /device:TPU:0, one launch (start us, length us, event | category | flops | bytes accessed | tf_op | source)
XLA Modules:
  0.0 220.7 jit_solution(7567981317895701346)
XLA Ops:
  0.1 7.4 %reshape.96 = bf16[1024,2048]{1,0:T(8,128)(2,1)} reshape(bf16[128,16384]{1,0:T(8,128)(2,1)} %param.5) | data formatting | bytes 8388608 | tf_op jit(solution)/shard_map/reshape | solution.py:75
  7.6 3.7 %multiply_reduce_fusion = (f32[1024]{0:T(1024)S(1)}, f32[1024,128]{0,1:T(8,128)S(1)}) fusion(bf16[2048,128]{1,0:T(8,128)(2,1)S(1)} %bitcast.40, bf16[1024,2048]{1,0:T(8,128)(2,1)} %reshape.96), kind=kOutput, calls=%fused_computation.14 | convolution fusion | flops 537132032 | bytes 5246976 | tf_op jit(solution)/shard_map/dot_general | solution.py:76
  11.9 2.6 %broadcast_in_dim.29 = bf16[2048,1024]{1,0:T(8,128)(2,1)} broadcast(bf16[]{:T(256)} %constant.207.clone.1), dimensions={} | broadcast | bytes 4194306 | tf_op jit(solution)/shard_map/broadcast_in_dim | solution.py:16
  15.8 5.0 %collective-permute-start.1 = (bf16[128,1024]{1,0:T(8,128)(2,1)S(1)}, bf16[128,1024]{1,0:T(8,128)(2,1)S(1)}, u32[]{:S(2)}, u32[]{:S(2)}) collective-permute-start(bf16[128,1024]{1,0:T(8,128)(2,1)S(1)} %get-tuple-element.143), channel_id=1, source_target_pairs={{0,15},{1,0},{2,1},{3,2},{4,3},{5,4},{6,5},{7,6},{8,7},{9,8},{10,9... | collective-permute-start | bytes 786440 | tf_op jit(solution)/shard_map/ppermute | solution.py:30
  20.7 4.2 %collective-permute-done = bf16[128,1024]{1,0:T(8,128)(2,1)S(1)} collective-permute-done((bf16[128,1024]{1,0:T(8,128)(2,1)S(1)}, bf16[128,1024]{1,0:T(8,128)(2,1)S(1)}, u32[]{:S(2)}, u32[]{:S(2)}) %collective-permute-start) | collective-permute-done | bytes 262176 | tf_op jit(solution)/shard_map/ppermute | solution.py:23
  24.9 4.4 %collective-permute-start.3 = (bf16[128,1024]{1,0:T(8,128)(2,1)S(1)}, bf16[128,1024]{1,0:T(8,128)(2,1)S(1)}, u32[]{:S(2)}, u32[]{:S(2)}) collective-permute-start(bf16[128,1024]{1,0:T(8,128)(2,1)S(1)} %collective-permute-done.1), channel_id=1, source_target_pairs={{0,15},{1,0},{2,1},{3,2},{4,3},{5,4},{6,5},{7,6},{8,7},{9,8},{10,9... | collective-permute-start | bytes 786440 | tf_op jit(solution)/shard_map/ppermute | solution.py:30
  29.3 4.2 %collective-permute-done.2 = bf16[128,1024]{1,0:T(8,128)(2,1)S(1)} collective-permute-done((bf16[128,1024]{1,0:T(8,128)(2,1)S(1)}, bf16[128,1024]{1,0:T(8,128)(2,1)S(1)}, u32[]{:S(2)}, u32[]{:S(2)}) %collective-permute-start.2) | collective-permute-done | bytes 262176 | tf_op jit(solution)/shard_map/ppermute | solution.py:23
  33.5 4.5 %collective-permute-start.5 = (bf16[128,1024]{1,0:T(8,128)(2,1)S(1)}, bf16[128,1024]{1,0:T(8,128)(2,1)S(1)}, u32[]{:S(2)}, u32[]{:S(2)}) collective-permute-start(bf16[128,1024]{1,0:T(8,128)(2,1)S(1)} %collective-permute-done.3), channel_id=1, source_target_pairs={{0,15},{1,0},{2,1},{3,2},{4,3},{5,4},{6,5},{7,6},{8,7},{9,8},{10,9... | collective-permute-start | bytes 786440 | tf_op jit(solution)/shard_map/ppermute | solution.py:30
  38.0 4.1 %collective-permute-done.4 = bf16[128,1024]{1,0:T(8,128)(2,1)S(1)} collective-permute-done((bf16[128,1024]{1,0:T(8,128)(2,1)S(1)}, bf16[128,1024]{1,0:T(8,128)(2,1)S(1)}, u32[]{:S(2)}, u32[]{:S(2)}) %collective-permute-start.4) | collective-permute-done | bytes 262176 | tf_op jit(solution)/shard_map/ppermute | solution.py:23
  43.2 4.2 %collective-permute-start.7 = (bf16[128,1024]{1,0:T(8,128)(2,1)S(1)}, bf16[128,1024]{1,0:T(8,128)(2,1)S(1)}, u32[]{:S(2)}, u32[]{:S(2)}) collective-permute-start(bf16[128,1024]{1,0:T(8,128)(2,1)S(1)} %collective-permute-done.5), channel_id=1, source_target_pairs={{0,15},{1,0},{2,1},{3,2},{4,3},{5,4},{6,5},{7,6},{8,7},{9,8},{10,9... | collective-permute-start | bytes 786440 | tf_op jit(solution)/shard_map/ppermute | solution.py:30
  48.1 2.6 %collective-permute-done.6 = bf16[128,1024]{1,0:T(8,128)(2,1)S(1)} collective-permute-done((bf16[128,1024]{1,0:T(8,128)(2,1)S(1)}, bf16[128,1024]{1,0:T(8,128)(2,1)S(1)}, u32[]{:S(2)}, u32[]{:S(2)}) %collective-permute-start.6) | collective-permute-done | bytes 262176 | tf_op jit(solution)/shard_map/ppermute | solution.py:23
  52.1 4.5 %collective-permute-start.9 = (bf16[128,1024]{1,0:T(8,128)(2,1)S(1)}, bf16[128,1024]{1,0:T(8,128)(2,1)S(1)}, u32[]{:S(2)}, u32[]{:S(2)}) collective-permute-start(bf16[128,1024]{1,0:T(8,128)(2,1)S(1)} %collective-permute-done.7), channel_id=1, source_target_pairs={{0,15},{1,0},{2,1},{3,2},{4,3},{5,4},{6,5},{7,6},{8,7},{9,8},{10,9... | collective-permute-start | bytes 786440 | tf_op jit(solution)/shard_map/ppermute | solution.py:30
  57.3 1.9 collective-permute-done.8
  60.8 4.5 %collective-permute-start.11 = (bf16[128,1024]{1,0:T(8,128)(2,1)S(1)}, bf16[128,1024]{1,0:T(8,128)(2,1)S(1)}, u32[]{:S(2)}, u32[]{:S(2)}) collective-permute-start(bf16[128,1024]{1,0:T(8,128)(2,1)S(1)} %collective-permute-done.9), channel_id=1, source_target_pairs={{0,15},{1,0},{2,1},{3,2},{4,3},{5,4},{6,5},{7,6},{8,7},{9,8},{10,9... | collective-permute-start | bytes 786440 | tf_op jit(solution)/shard_map/ppermute | solution.py:30
  65.9 2.0 collective-permute-done.10
  69.3 4.5 %collective-permute-start.13 = (bf16[128,1024]{1,0:T(8,128)(2,1)S(1)}, bf16[128,1024]{1,0:T(8,128)(2,1)S(1)}, u32[]{:S(2)}, u32[]{:S(2)}) collective-permute-start(bf16[128,1024]{1,0:T(8,128)(2,1)S(1)} %collective-permute-done.11), channel_id=1, source_target_pairs={{0,15},{1,0},{2,1},{3,2},{4,3},{5,4},{6,5},{7,6},{8,7},{9,8},{10,9... | collective-permute-start | bytes 786440 | tf_op jit(solution)/shard_map/ppermute | solution.py:30
  74.5 2.0 collective-permute-done.12
  78.7 6.3 %collective-permute-done.14 = bf16[128,1024]{1,0:T(8,128)(2,1)S(1)} collective-permute-done((bf16[128,1024]{1,0:T(8,128)(2,1)S(1)}, bf16[128,1024]{1,0:T(8,128)(2,1)S(1)}, u32[]{:S(2)}, u32[]{:S(2)}) %collective-permute-start.14) | collective-permute-done | bytes 262176 | tf_op jit(solution)/shard_map/ppermute | solution.py:23
  85.7 13.7 %gather_fusion = bf16[2048,1024]{1,0:T(8,128)(2,1)} fusion(bf16[2048,1024]{1,0:T(8,128)(2,1)} %constant_dynamic-update-slice_fusion, s32[2048]{0:T(1024)S(1)} %fusion.3), kind=kCustom, calls=%fused_computation | custom fusion | bytes 8396800 | tf_op jit(solution)/shard_map/jit(_take)/gather | solution.py:84
  99.5 2.5 %broadcast_select_fusion = bf16[2048,1024]{1,0:T(8,128)(2,1)S(1)} fusion(bf16[2048,1024]{1,0:T(8,128)(2,1)} %gather_fusion, pred[2048]{0:T(1024)(128)(4,1)S(1)} %compare_and_fusion), kind=kLoop, calls=%fused_computation.9 | loop fusion | flops 2097152 | bytes 8390656 | tf_op jit(solution)/shard_map/jit(_take)/select_n | solution.py:84
  102.0 2.0 copy-done
  104.2 33.3 %while.17 = (s32[]{:T(128)}, bf16[128,1152]{1,0:T(8,128)(2,1)S(1)}, s32[17,2]{0,1:T(2,128)S(1)}, bf16[17,128,1024]{2,1,0:T(8,128)(2,1)}, s32[]{:T(128)}) while((s32[]{:T(128)}, bf16[128,1152]{1,0:T(8,128)(2,1)S(1)}, s32[17,2]{0,1:T(2,128)S(1)}, bf16[17,128,1024]{2,1,0:T(8,128)(2,1)}, s32[]{:T(128)}) %tuple.53), condition=%wide.while_cond, body=%wide.while_body.sunk | while | flops 2 | bytes 525401 | solution.py:51
  104.8 1.4 bitcast_dynamic-update-slice_fusion.8
  106.7 1.4 bitcast_dynamic-update-slice_fusion.8
  108.7 1.4 bitcast_dynamic-update-slice_fusion.8
  110.7 1.4 bitcast_dynamic-update-slice_fusion.8
  112.6 1.4 bitcast_dynamic-update-slice_fusion.8
  114.6 1.4 bitcast_dynamic-update-slice_fusion.8
  116.5 1.4 bitcast_dynamic-update-slice_fusion.8
  118.5 1.4 bitcast_dynamic-update-slice_fusion.8
  120.5 1.4 bitcast_dynamic-update-slice_fusion.8
  122.4 1.4 bitcast_dynamic-update-slice_fusion.8
  124.4 1.4 bitcast_dynamic-update-slice_fusion.8
  126.4 1.4 bitcast_dynamic-update-slice_fusion.8
  128.3 1.4 bitcast_dynamic-update-slice_fusion.8
  130.3 1.4 bitcast_dynamic-update-slice_fusion.8
  132.2 1.4 bitcast_dynamic-update-slice_fusion.8
  136.1 1.4 bitcast_dynamic-update-slice_fusion.8
  137.5 4.8 %pad_maximum_fusion = bf16[2176,1024]{1,0:T(8,128)(2,1)} fusion(bf16[128,1024]{1,0:T(8,128)(2,1)S(1)} %get-tuple-element.147, bf16[2048,1024]{1,0:T(8,128)(2,1)} %copy-done), kind=kLoop, calls=%fused_computation.8 | loop fusion | flops 8912896 | bytes 8912896 | tf_op jit(solution)/shard_map/concatenate | solution.py:90
  142.4 77.2 %while.16 = (s32[]{:T(128)}, f32[16,128,128]{2,1,0:T(8,128)S(1)}, bf16[2176,1024]{1,0:T(8,128)(2,1)}, bf16[2176,1024]{1,0:T(8,128)(2,1)}, s32[]{:T(128)}, /*inde...) while((s32[]{:T(128)}, f32[16,128,128]{2,1,0:T(8,128)S(1)}, ...), condition=%wide.region_4.5_spmd, body=%wide.region_2.4_spmd.sunk | while | flops 1141374976 | bytes 19005812 | solution.py:98
  142.4 3.9 %convolution_bitcast_fusion.3 = f32[2176,256]{0,1:T(8,128)S(1)} fusion(bf16[2176,1024]{1,0:T(8,128)(2,1)} %get-tuple-element.246, bf16[2176,1024]{1,0:T(8,128)(2,1)} %get-tuple-element.245, s32[]{:T(128)S(6)} %select_n.222), kind=kOutput, calls=%fused_computation.1.clone.1 | convolution fusion | flops 1140850688 | bytes 7208964 | tf_op jit(solution)/shard_map/while/body/eval_jaxpr/dot_general | solution.py:61
  146.3 2.0 copy.14
  148.3 2.7 %reshape.129 = f32[17,128,2,128]{3,2,1,0:T(2,128)S(1)} reshape(f32[2176,256]{1,0:T(8,128)} %copy.14) | data formatting | bytes 4456448 | tf_op jit(solution)/shard_map/while/body/eval_jaxpr/reshape | solution.py:64
  152.1 3.9 %convolution_bitcast_fusion.3 = f32[2176,256]{0,1:T(8,128)S(1)} fusion(bf16[2176,1024]{1,0:T(8,128)(2,1)} %get-tuple-element.246, bf16[2176,1024]{1,0:T(8,128)(2,1)} %get-tuple-element.245, s32[]{:T(128)S(6)} %select_n.222), kind=kOutput, calls=%fused_computation.1.clone.1 | convolution fusion | flops 1140850688 | bytes 7208964 | tf_op jit(solution)/shard_map/while/body/eval_jaxpr/dot_general | solution.py:61
  155.9 2.0 copy.14
  157.9 2.7 %reshape.129 = f32[17,128,2,128]{3,2,1,0:T(2,128)S(1)} reshape(f32[2176,256]{1,0:T(8,128)} %copy.14) | data formatting | bytes 4456448 | tf_op jit(solution)/shard_map/while/body/eval_jaxpr/reshape | solution.py:64
  161.7 3.9 %convolution_bitcast_fusion.3 = f32[2176,256]{0,1:T(8,128)S(1)} fusion(bf16[2176,1024]{1,0:T(8,128)(2,1)} %get-tuple-element.246, bf16[2176,1024]{1,0:T(8,128)(2,1)} %get-tuple-element.245, s32[]{:T(128)S(6)} %select_n.222), kind=kOutput, calls=%fused_computation.1.clone.1 | convolution fusion | flops 1140850688 | bytes 7208964 | tf_op jit(solution)/shard_map/while/body/eval_jaxpr/dot_general | solution.py:61
  165.6 2.0 copy.14
  167.6 2.7 %reshape.129 = f32[17,128,2,128]{3,2,1,0:T(2,128)S(1)} reshape(f32[2176,256]{1,0:T(8,128)} %copy.14) | data formatting | bytes 4456448 | tf_op jit(solution)/shard_map/while/body/eval_jaxpr/reshape | solution.py:64
  171.4 3.9 %convolution_bitcast_fusion.3 = f32[2176,256]{0,1:T(8,128)S(1)} fusion(bf16[2176,1024]{1,0:T(8,128)(2,1)} %get-tuple-element.246, bf16[2176,1024]{1,0:T(8,128)(2,1)} %get-tuple-element.245, s32[]{:T(128)S(6)} %select_n.222), kind=kOutput, calls=%fused_computation.1.clone.1 | convolution fusion | flops 1140850688 | bytes 7208964 | tf_op jit(solution)/shard_map/while/body/eval_jaxpr/dot_general | solution.py:61
  175.2 2.0 copy.14
  177.2 2.7 %reshape.129 = f32[17,128,2,128]{3,2,1,0:T(2,128)S(1)} reshape(f32[2176,256]{1,0:T(8,128)} %copy.14) | data formatting | bytes 4456448 | tf_op jit(solution)/shard_map/while/body/eval_jaxpr/reshape | solution.py:64
  181.0 3.9 %convolution_bitcast_fusion.3 = f32[2176,256]{0,1:T(8,128)S(1)} fusion(bf16[2176,1024]{1,0:T(8,128)(2,1)} %get-tuple-element.246, bf16[2176,1024]{1,0:T(8,128)(2,1)} %get-tuple-element.245, s32[]{:T(128)S(6)} %select_n.222), kind=kOutput, calls=%fused_computation.1.clone.1 | convolution fusion | flops 1140850688 | bytes 7208964 | tf_op jit(solution)/shard_map/while/body/eval_jaxpr/dot_general | solution.py:61
  184.9 2.0 copy.14
  186.9 2.7 %reshape.129 = f32[17,128,2,128]{3,2,1,0:T(2,128)S(1)} reshape(f32[2176,256]{1,0:T(8,128)} %copy.14) | data formatting | bytes 4456448 | tf_op jit(solution)/shard_map/while/body/eval_jaxpr/reshape | solution.py:64
  190.7 3.9 %convolution_bitcast_fusion.3 = f32[2176,256]{0,1:T(8,128)S(1)} fusion(bf16[2176,1024]{1,0:T(8,128)(2,1)} %get-tuple-element.246, bf16[2176,1024]{1,0:T(8,128)(2,1)} %get-tuple-element.245, s32[]{:T(128)S(6)} %select_n.222), kind=kOutput, calls=%fused_computation.1.clone.1 | convolution fusion | flops 1140850688 | bytes 7208964 | tf_op jit(solution)/shard_map/while/body/eval_jaxpr/dot_general | solution.py:61
  194.5 2.0 copy.14
  196.5 2.7 %reshape.129 = f32[17,128,2,128]{3,2,1,0:T(2,128)S(1)} reshape(f32[2176,256]{1,0:T(8,128)} %copy.14) | data formatting | bytes 4456448 | tf_op jit(solution)/shard_map/while/body/eval_jaxpr/reshape | solution.py:64
  200.3 3.9 %convolution_bitcast_fusion.3 = f32[2176,256]{0,1:T(8,128)S(1)} fusion(bf16[2176,1024]{1,0:T(8,128)(2,1)} %get-tuple-element.246, bf16[2176,1024]{1,0:T(8,128)(2,1)} %get-tuple-element.245, s32[]{:T(128)S(6)} %select_n.222), kind=kOutput, calls=%fused_computation.1.clone.1 | convolution fusion | flops 1140850688 | bytes 7208964 | tf_op jit(solution)/shard_map/while/body/eval_jaxpr/dot_general | solution.py:61
  204.2 2.0 copy.14
  206.2 2.7 %reshape.129 = f32[17,128,2,128]{3,2,1,0:T(2,128)S(1)} reshape(f32[2176,256]{1,0:T(8,128)} %copy.14) | data formatting | bytes 4456448 | tf_op jit(solution)/shard_map/while/body/eval_jaxpr/reshape | solution.py:64
  210.0 3.9 %convolution_bitcast_fusion.3 = f32[2176,256]{0,1:T(8,128)S(1)} fusion(bf16[2176,1024]{1,0:T(8,128)(2,1)} %get-tuple-element.246, bf16[2176,1024]{1,0:T(8,128)(2,1)} %get-tuple-element.245, s32[]{:T(128)S(6)} %select_n.222), kind=kOutput, calls=%fused_computation.1.clone.1 | convolution fusion | flops 1140850688 | bytes 7208964 | tf_op jit(solution)/shard_map/while/body/eval_jaxpr/dot_general | solution.py:61
  213.8 2.0 copy.14
  215.8 2.7 %reshape.129 = f32[17,128,2,128]{3,2,1,0:T(2,128)S(1)} reshape(f32[2176,256]{1,0:T(8,128)} %copy.14) | data formatting | bytes 4456448 | tf_op jit(solution)/shard_map/while/body/eval_jaxpr/reshape | solution.py:64
  (120 shorter events, 33.0 us)
Async XLA Ops:
  11.4 22.1 %copy-start.1 = (s32[2048]{0:T(1024)S(1)}, s32[2048]{0:T(1024)}, u32[]{:S(2)}) copy-start(s32[2048]{0:T(1024)} %param.6) | copy-start | bytes 24580
  11.4 30.7 %copy-start.2 = (s32[17]{0:T(128)S(1)}, s32[17]{0:T(128)}, u32[]{:S(2)}) copy-start(s32[17]{0:T(128)} %param.7) | copy-start | bytes 208
  15.3 9.6 %collective-permute-start = (bf16[128,1024]{1,0:T(8,128)(2,1)S(1)}, bf16[128,1024]{1,0:T(8,128)(2,1)S(1)}, u32[]{:S(2)}, u32[]{:S(2)}) collective-permute-start(bf16[128,1024]{1,0:T(8,128)(2,1)S(1)} %get-tuple-element.143), channel_id=1, source_target_pairs={{0,1},{1,2},{2,3},{3,4},{4,5},{5,6},{6,7},{7,8},{8,9},{9,10},{10,1... | collective-permute-start | bytes 786440 | tf_op jit(solution)/shard_map/ppermute | solution.py:23
  15.8 9.1 %collective-permute-start.1 = (bf16[128,1024]{1,0:T(8,128)(2,1)S(1)}, bf16[128,1024]{1,0:T(8,128)(2,1)S(1)}, u32[]{:S(2)}, u32[]{:S(2)}) collective-permute-start(bf16[128,1024]{1,0:T(8,128)(2,1)S(1)} %get-tuple-element.143), channel_id=1, source_target_pairs={{0,15},{1,0},{2,1},{3,2},{4,3},{5,4},{6,5},{7,6},{8,7},{9,8},{10,9... | collective-permute-start | bytes 786440 | tf_op jit(solution)/shard_map/ppermute | solution.py:30
  24.9 8.6 %collective-permute-start.2 = (bf16[128,1024]{1,0:T(8,128)(2,1)S(1)}, bf16[128,1024]{1,0:T(8,128)(2,1)S(1)}, u32[]{:S(2)}, u32[]{:S(2)}) collective-permute-start(bf16[128,1024]{1,0:T(8,128)(2,1)S(1)} %collective-permute-done), channel_id=1, source_target_pairs={{0,1},{1,2},{2,3},{3,4},{4,5},{5,6},{6,7},{7,8},{8,9},{9,10},{10,1... | collective-permute-start | bytes 786440 | tf_op jit(solution)/shard_map/ppermute | solution.py:23
  24.9 8.6 %collective-permute-start.3 = (bf16[128,1024]{1,0:T(8,128)(2,1)S(1)}, bf16[128,1024]{1,0:T(8,128)(2,1)S(1)}, u32[]{:S(2)}, u32[]{:S(2)}) collective-permute-start(bf16[128,1024]{1,0:T(8,128)(2,1)S(1)} %collective-permute-done.1), channel_id=1, source_target_pairs={{0,15},{1,0},{2,1},{3,2},{4,3},{5,4},{6,5},{7,6},{8,7},{9,8},{10,9... | collective-permute-start | bytes 786440 | tf_op jit(solution)/shard_map/ppermute | solution.py:30
  33.5 8.6 %collective-permute-start.4 = (bf16[128,1024]{1,0:T(8,128)(2,1)S(1)}, bf16[128,1024]{1,0:T(8,128)(2,1)S(1)}, u32[]{:S(2)}, u32[]{:S(2)}) collective-permute-start(bf16[128,1024]{1,0:T(8,128)(2,1)S(1)} %collective-permute-done.2), channel_id=1, source_target_pairs={{0,1},{1,2},{2,3},{3,4},{4,5},{5,6},{6,7},{7,8},{8,9},{9,10},{10,1... | collective-permute-start | bytes 786440 | tf_op jit(solution)/shard_map/ppermute | solution.py:23
  33.5 9.7 %collective-permute-start.5 = (bf16[128,1024]{1,0:T(8,128)(2,1)S(1)}, bf16[128,1024]{1,0:T(8,128)(2,1)S(1)}, u32[]{:S(2)}, u32[]{:S(2)}) collective-permute-start(bf16[128,1024]{1,0:T(8,128)(2,1)S(1)} %collective-permute-done.3), channel_id=1, source_target_pairs={{0,15},{1,0},{2,1},{3,2},{4,3},{5,4},{6,5},{7,6},{8,7},{9,8},{10,9... | collective-permute-start | bytes 786440 | tf_op jit(solution)/shard_map/ppermute | solution.py:30
  42.1 8.6 %collective-permute-start.6 = (bf16[128,1024]{1,0:T(8,128)(2,1)S(1)}, bf16[128,1024]{1,0:T(8,128)(2,1)S(1)}, u32[]{:S(2)}, u32[]{:S(2)}) collective-permute-start(bf16[128,1024]{1,0:T(8,128)(2,1)S(1)} %collective-permute-done.4), channel_id=1, source_target_pairs={{0,1},{1,2},{2,3},{3,4},{4,5},{5,6},{6,7},{7,8},{8,9},{9,10},{10,1... | collective-permute-start | bytes 786440 | tf_op jit(solution)/shard_map/ppermute | solution.py:23
  43.2 9.0 %collective-permute-start.7 = (bf16[128,1024]{1,0:T(8,128)(2,1)S(1)}, bf16[128,1024]{1,0:T(8,128)(2,1)S(1)}, u32[]{:S(2)}, u32[]{:S(2)}) collective-permute-start(bf16[128,1024]{1,0:T(8,128)(2,1)S(1)} %collective-permute-done.5), channel_id=1, source_target_pairs={{0,15},{1,0},{2,1},{3,2},{4,3},{5,4},{6,5},{7,6},{8,7},{9,8},{10,9... | collective-permute-start | bytes 786440 | tf_op jit(solution)/shard_map/ppermute | solution.py:30
  50.7 8.6 %collective-permute-start.8 = (bf16[128,1024]{1,0:T(8,128)(2,1)S(1)}, bf16[128,1024]{1,0:T(8,128)(2,1)S(1)}, u32[]{:S(2)}, u32[]{:S(2)}) collective-permute-start(bf16[128,1024]{1,0:T(8,128)(2,1)S(1)} %collective-permute-done.6), channel_id=1, source_target_pairs={{0,1},{1,2},{2,3},{3,4},{4,5},{5,6},{6,7},{7,8},{8,9},{9,10},{10,1... | collective-permute-start | bytes 786440 | tf_op jit(solution)/shard_map/ppermute | solution.py:23
  52.1 8.6 %collective-permute-start.9 = (bf16[128,1024]{1,0:T(8,128)(2,1)S(1)}, bf16[128,1024]{1,0:T(8,128)(2,1)S(1)}, u32[]{:S(2)}, u32[]{:S(2)}) collective-permute-start(bf16[128,1024]{1,0:T(8,128)(2,1)S(1)} %collective-permute-done.7), channel_id=1, source_target_pairs={{0,15},{1,0},{2,1},{3,2},{4,3},{5,4},{6,5},{7,6},{8,7},{9,8},{10,9... | collective-permute-start | bytes 786440 | tf_op jit(solution)/shard_map/ppermute | solution.py:30
  59.3 8.6 %collective-permute-start.10 = (bf16[128,1024]{1,0:T(8,128)(2,1)S(1)}, bf16[128,1024]{1,0:T(8,128)(2,1)S(1)}, u32[]{:S(2)}, u32[]{:S(2)}) collective-permute-start(bf16[128,1024]{1,0:T(8,128)(2,1)S(1)} %collective-permute-done.8), channel_id=1, source_target_pairs={{0,1},{1,2},{2,3},{3,4},{4,5},{5,6},{6,7},{7,8},{8,9},{9,10},{10,1... | collective-permute-start | bytes 786440 | tf_op jit(solution)/shard_map/ppermute | solution.py:23
  60.8 8.6 %collective-permute-start.11 = (bf16[128,1024]{1,0:T(8,128)(2,1)S(1)}, bf16[128,1024]{1,0:T(8,128)(2,1)S(1)}, u32[]{:S(2)}, u32[]{:S(2)}) collective-permute-start(bf16[128,1024]{1,0:T(8,128)(2,1)S(1)} %collective-permute-done.9), channel_id=1, source_target_pairs={{0,15},{1,0},{2,1},{3,2},{4,3},{5,4},{6,5},{7,6},{8,7},{9,8},{10,9... | collective-permute-start | bytes 786440 | tf_op jit(solution)/shard_map/ppermute | solution.py:30
  67.9 8.6 %collective-permute-start.12 = (bf16[128,1024]{1,0:T(8,128)(2,1)S(1)}, bf16[128,1024]{1,0:T(8,128)(2,1)S(1)}, u32[]{:S(2)}, u32[]{:S(2)}) collective-permute-start(bf16[128,1024]{1,0:T(8,128)(2,1)S(1)} %collective-permute-done.10), channel_id=1, source_target_pairs={{0,1},{1,2},{2,3},{3,4},{4,5},{5,6},{6,7},{7,8},{8,9},{9,10},{10,1... | collective-permute-start | bytes 786440 | tf_op jit(solution)/shard_map/ppermute | solution.py:23
  69.3 8.6 %collective-permute-start.13 = (bf16[128,1024]{1,0:T(8,128)(2,1)S(1)}, bf16[128,1024]{1,0:T(8,128)(2,1)S(1)}, u32[]{:S(2)}, u32[]{:S(2)}) collective-permute-start(bf16[128,1024]{1,0:T(8,128)(2,1)S(1)} %collective-permute-done.11), channel_id=1, source_target_pairs={{0,15},{1,0},{2,1},{3,2},{4,3},{5,4},{6,5},{7,6},{8,7},{9,8},{10,9... | collective-permute-start | bytes 786440 | tf_op jit(solution)/shard_map/ppermute | solution.py:30
  76.5 8.5 %collective-permute-start.14 = (bf16[128,1024]{1,0:T(8,128)(2,1)S(1)}, bf16[128,1024]{1,0:T(8,128)(2,1)S(1)}, u32[]{:S(2)}, u32[]{:S(2)}) collective-permute-start(bf16[128,1024]{1,0:T(8,128)(2,1)S(1)} %collective-permute-done.12), channel_id=1, source_target_pairs={{0,1},{1,2},{2,3},{3,4},{4,5},{5,6},{6,7},{7,8},{8,9},{9,10},{10,1... | collective-permute-start | bytes 786440 | tf_op jit(solution)/shard_map/ppermute | solution.py:23
  102.0 2.0 copy-start
